TPU v7x, 256 devices: a whole 4x4x8 slice. The times are simulated.
256 devices in a mesh: ray: 16 (over y, z_lo), pix: 16 (over z_hi, x, core).
Axes of the slice: x: 4, y: 4, z: 8 (z_hi: 2, z_lo: 4; z = z_hi * 4 + z_lo), core: 2. Of those that a mesh axis runs over, the one named last changes fastest.
Arguments:
- positions: float32 [2, 16384], P(None, 'ray'), may hold values from -2 to 2
- directions: float32 [2, 16384], P(None, 'ray'), may hold values from -0.35 to 0.35
- path: float32 [16384], P('ray'), may hold values from -9 to 9
- amplitude: float32 [16384], P('ray'), may hold values from 0.3 to 3
- psf_grad: float32 [3, 1024, 1024], P(None, 'pix', 'ray'), may hold values from -0.3 to 0.3
Outputs:
- psf: float32 [3, 1024, 1024], P(None, 'pix', 'ray')
- ray_grad: float32 [6, 16384], P(None, 'ray')
All inputs are finite; a program needn't handle non-finite values.
Results may differ from a plain program's by a relative error of at most 0.0054.
Values may be sent and summed in bfloat16 or wider, within the bound.
A program may use at most 192 MiB of HBM per device.

v0:
```python
import math
import jax
import jax.numpy as jnp
from jax import lax
from jax.sharding import PartitionSpec as P

NPIX = 1024
wave_scales = (1.2088, 1.0, 0.8953)
two_pi = 2.0 * math.pi


def centred(start, count):
    return (start + jnp.arange(count)).astype(jnp.float32) - 0.5 * NPIX + 0.5


def build_tables(rays, rows_x, cols_y, norm):
    row_list = []
    col_list = []
    weight = (rays[5] * norm)[:, None]
    for wave in range(3):
        scale = wave_scales[wave]
        angle = scale * (
            rays[4][:, None]
            + two_pi
            * (
                rays[2][:, None] * (rows_x[None, :] - rays[0][:, None])
                - rays[3][:, None] * rays[1][:, None]
            )
        )
        row_list.append(jnp.stack([weight * jnp.cos(angle), weight * jnp.sin(angle)]))
        beta = scale * two_pi * cols_y[:, None] * rays[3][None, :]
        col_list.append(jnp.stack([jnp.cos(beta), jnp.sin(beta)]))
    return (jnp.stack(row_list), jnp.stack(col_list))


def mixing(a_re, a_im):
    upper = jnp.concatenate([a_re, a_im], axis=1)
    lower = jnp.concatenate([-a_im, a_re], axis=1)
    return jnp.concatenate([upper, lower], axis=0).astype(jnp.bfloat16)


def product(left, right, dims):
    return lax.dot_general(left, right, dims, preferred_element_type=jnp.float32)


def block_count(count):
    return max(1, min(16, count // 256))


def field_terms(row_tab, col_tab):
    count = row_tab.shape[2]
    nblk = block_count(count)
    blk = count // nblk

    def step(index, total):
        a_blk = lax.dynamic_slice_in_dim(row_tab, index * blk, blk, 2)
        b_blk = lax.dynamic_slice_in_dim(col_tab, index * blk, blk, 3)
        parts = []
        for wave in range(3):
            left = jnp.concatenate([b_blk[wave, 0], b_blk[wave, 1]], axis=1).astype(jnp.bfloat16)
            parts.append(
                product(left, mixing(a_blk[wave, 0], a_blk[wave, 1]), (((1,), (0,)), ((), ())))
            )
        return total + jnp.concatenate(parts, axis=1)

    init = jnp.zeros((col_tab.shape[2], 6 * row_tab.shape[3]), jnp.float32)
    return lax.fori_loop(0, nblk, step, init)


def ray_partials(row_tab, col_tab, rows_x, cols_y, cotangent):
    count = row_tab.shape[2]
    nblk = block_count(count)
    blk = count // nblk
    plen = rows_x.shape[0]

    def one_block(index):
        a_blk = lax.dynamic_slice_in_dim(row_tab, index * blk, blk, 2)
        b_blk = lax.dynamic_slice_in_dim(col_tab, index * blk, blk, 3)
        first = jnp.zeros((blk,), jnp.float32)
        second = jnp.zeros((blk,), jnp.float32)
        third = jnp.zeros((blk,), jnp.float32)
        fourth = jnp.zeros((blk,), jnp.float32)
        for wave in range(3):
            scale = wave_scales[wave]
            a_re = a_blk[wave, 0]
            a_im = a_blk[wave, 1]
            b_re = b_blk[wave, 0]
            b_im = b_blk[wave, 1]
            left = jnp.concatenate([b_re, b_im], axis=1).astype(jnp.bfloat16)
            mix = mixing(a_re, a_im)
            grad_u = cotangent[:, 2 * plen * wave : 2 * plen * (wave + 1)]
            proj = product(left, grad_u, (((0,), (0,)), ((), ())))
            d_are = proj[:blk, :plen] + proj[blk:, plen:]
            d_aim = proj[:blk, plen:] - proj[blk:, :plen]
            d_b = product(grad_u, mix, (((1,), (1,)), ((), ())))
            d_beta = d_b[:, blk:] * b_re - d_b[:, :blk] * b_im
            d_alpha = d_aim * a_re - d_are * a_im
            first = first + scale * jnp.sum(d_alpha, axis=1)
            second = second + scale * two_pi * jnp.sum(d_alpha * rows_x[None, :], axis=1)
            third = third + scale * two_pi * jnp.sum(d_beta * cols_y[:, None], axis=0)
            fourth = fourth + jnp.sum(d_are * a_re + d_aim * a_im, axis=1)
        return jnp.stack([first, second, third, fourth])

    out = lax.map(one_block, jnp.arange(nblk))
    return jnp.transpose(out, (1, 0, 2)).reshape(4, count)


def finish(sums, rays):
    return jnp.stack(
        [
            sums[0],
            -two_pi * rays[2] * sums[0],
            -two_pi * rays[3] * sums[0],
            (sums[1] - two_pi * rays[0] * sums[0]) / NPIX,
            (sums[2] - two_pi * rays[1] * sums[0]) / NPIX,
            sums[3] / rays[5],
        ]
    )


def intensity(field, psf_grad, clen, plen):
    shaped = field.reshape(clen, 3, 2, plen)
    psf = jnp.transpose(shaped[:, :, 0] ** 2 + shaped[:, :, 1] ** 2, (1, 2, 0))
    weight = jnp.transpose(psf_grad, (2, 0, 1))
    grad_u = (2.0 * weight[:, :, None, :] * shaped).reshape(clen, 6 * plen).astype(jnp.bfloat16)
    return (psf, grad_u)


def on_device(positions, directions, path, amplitude, psf_grad):
    rays = jnp.concatenate([positions, directions, path[None], amplitude[None]], axis=0)
    local = rays.shape[1]
    plen = NPIX // lax.axis_size("pix")
    clen = NPIX // lax.axis_size("ray")
    norm = 1.0 / math.sqrt(local * lax.axis_size("ray"))
    rows_x = centred(lax.axis_index("pix") * plen, plen)
    all_cols = centred(0, NPIX)
    row_tab, col_tab = build_tables(rays, rows_x, all_cols, norm)
    field = lax.psum_scatter(field_terms(row_tab, col_tab), "ray", scatter_dimension=0, tiled=True)
    psf, grad_u = intensity(field, psf_grad, clen, plen)
    gathered = lax.all_gather(grad_u, "ray", axis=0, tiled=True)
    partial_value = ray_partials(row_tab, col_tab, rows_x, all_cols, gathered)
    sums = lax.psum(partial_value, "pix")
    return (psf, finish(sums, rays))


def solution(mesh):
    in_specs = (P(None, "ray"), P(None, "ray"), P("ray"), P("ray"), P(None, "pix", "ray"))
    out_specs = (P(None, "pix", "ray"), P(None, "ray"))
    return jax.shard_map(
        on_device, mesh=mesh, in_specs=in_specs, out_specs=out_specs, check_vma=False
    )
```

profile of v0, /device:TPU:32, one launch (start us, length us, event | category | flops | bytes accessed | tf_op | source)
XLA Modules:
  0.0 497.8 jit_solution(16539537502296417018)
XLA Ops:
  9.5 3.6 cosine_multiply_fusion.2
  13.2 46.6 %multiply_cosine_fusion.2 = (f32[1,1024,1024]{2,1,0:T(8,128)}, f32[1,1024,1024]{2,1,0:T(8,128)}, f32[1,1024,1024]{2,1,0:T(8,128)}, f32[1,1024,1024]{2,1,0:T(8,12...) fusion(f32[1024]{0:T(1024)S(1)} %bitcast.214, f32[1024]{0:T(1024)S(1)} %fusion.111, ...), kind=kLoop, calls=%fused_computation.186 | loop fusion | flops 3145728 | bytes 25182208 | tf_op jit(solution)/shard_map/cos | solution.py:32
  62.8 9.3 %maximum_bitcast_fusion.1 = (f32[1,2,1024,1024]{3,2,1,0:T(8,128)S(1)}, f32[1,2,1024,1024]{3,2,1,0:T(8,128)}) fusion(f32[1,1024,1024]{2,1,0:T(8,128)} %get-tuple-element.336, f32[1,1024,1024]{2,1,0:T(8,128)} %get-tuple-element.335, f32[1,1024,1024]{2,1,0:T(8,128)} %get-tuple-element.341, f32[1,1024,1024]{2,1,0:T(8,128)} %get-tuple-element.342), kind=kLoop, calls=%fused_computation.178 | loop fusion | flops 4194304 | bytes 33554432 | tf_op jit(solution)/shard_map/stack | solution.py:33
  72.1 15.7 %fusion.115 = (bf16[3,2,1024,1024]{3,2,1,0:T(8,128)(2,1)}, f32[3,2,1024,1024]{3,2,1,0:T(8,128)}) fusion(f32[1,2,1024,1024]{3,2,1,0:T(8,128)S(1)} %maximum_bitcast_fusion.3, f32[1,2,1024,1024]{3,2,1,0:T(8,128)} %get-tuple-element.346, f32[1,2,1024,1024]{3,2,1,0:T(8,128)S(1)} %get-tuple-element.345), kind=kLoop, calls=%fused_computation.219 | loop fusion | flops 18874368 | bytes 62914560
  87.8 56.3 %while.27 = (s32[]{:T(128)}, f32[1024,384]{0,1:T(8,128)S(1)}, bf16[3,2,1024,1024]{3,2,1,0:T(8,128)(2,1)}, f32[3,2,1024,64]{2,3,1,0:T(8,128)}, s32[]{:T(128)}, /*...) while((s32[]{:T(128)}, f32[1024,384]{0,1:T(8,128)S(1)}, bf16[3,2,1024,1024]{3,2,1,0:T(8,128)(2,1)}, ...), condition=%wide.region_1.0_spmd.clone, body=%wide.region_0.0_spmd.clone.sunk | while | flops 412237824 | bytes 23888080 | solution.py:67
  96.0 2.5 fusion.173
  110.1 2.5 fusion.173
  124.2 2.5 fusion.173
  138.2 2.5 fusion.173
  145.9 87.3 %reduce-scatter.4.cloned.1.call-done = f32[64,384]{1,0:T(8,128)} async-done(((f32[1024,384]{1,0:T(8,128)}), f32[64,384]{1,0:T(8,128)}) %reduce-scatter.4.cloned.1.call-update) | async-done | bytes 98320
  234.4 51.1 %all_gather.3 = bf16[1024,384]{1,0:T(8,128)(2,1)} all-gather(bf16[64,384]{1,0:T(8,128)(2,1)S(1)} %copy.31), channel_id=1, replica_groups=mesh['ray'=16,'pix'=16] {'ray'}, dimensions={0}, use_global_device_ids=true | all-gather | bytes 835584 | tf_op jit(solution)/shard_map/all_gather | solution.py:140
  285.5 118.7 %while.26 = (s32[]{:T(128)}, f32[4,4,256]{2,1,0:T(4,128)S(1)}, s32[4]{0:T(128)S(1)}, f32[3,2,1024,1024]{3,2,1,0:T(8,128)}, bf16[1024,384]{1,0:T(8,128)(2,1)}, /*...) while((s32[]{:T(128)}, f32[4,4,256]{2,1,0:T(4,128)S(1)}, ...), condition=%wide.region_16.17_spmd.clone.clone, body=%wide.region_3.16_spmd.clone.clone.sunk | while | flops 819468480 | bytes 79344528 | solution.py:104
  286.7 5.2 %constant_dynamic-slice_fusion.15 = (f32[1,1,1024,256]{3,2,1,0:T(8,128)S(1)}, f32[1,1,1024,256]{3,2,1,0:T(8,128)}, f32[1,1,1024,256]{3,2,1,0:T(8,128)}, f32[1,1,...) fusion(f32[3,2,1024,1024]{3,2,1,0:T(8,128)} %get-tuple-element.584, ...), kind=kLoop, calls=%fused_computation.102.clone.1 | loop fusion | bytes 12582924 | tf_op jit(solution)/shard_map/while/body/eval_jaxpr/slice | solution.py:87
  295.7 2.5 copy.70
  301.8 2.5 copy.67
  304.3 2.5 copy.68
  316.4 5.2 %constant_dynamic-slice_fusion.15 = (f32[1,1,1024,256]{3,2,1,0:T(8,128)S(1)}, f32[1,1,1024,256]{3,2,1,0:T(8,128)}, f32[1,1,1024,256]{3,2,1,0:T(8,128)}, f32[1,1,...) fusion(f32[3,2,1024,1024]{3,2,1,0:T(8,128)} %get-tuple-element.584, ...), kind=kLoop, calls=%fused_computation.102.clone.1 | loop fusion | bytes 12582924 | tf_op jit(solution)/shard_map/while/body/eval_jaxpr/slice | solution.py:87
  325.4 2.5 copy.70
  329.3 2.1 fusion.160
  331.5 2.5 copy.67
  334.0 2.5 copy.68
  346.1 5.2 %constant_dynamic-slice_fusion.15 = (f32[1,1,1024,256]{3,2,1,0:T(8,128)S(1)}, f32[1,1,1024,256]{3,2,1,0:T(8,128)}, f32[1,1,1024,256]{3,2,1,0:T(8,128)}, f32[1,1,...) fusion(f32[3,2,1024,1024]{3,2,1,0:T(8,128)} %get-tuple-element.584, ...), kind=kLoop, calls=%fused_computation.102.clone.1 | loop fusion | bytes 12582924 | tf_op jit(solution)/shard_map/while/body/eval_jaxpr/slice | solution.py:87
  355.1 2.5 copy.70
  359.0 2.1 fusion.160
  361.1 2.5 copy.67
  363.7 2.5 copy.68
  375.8 5.2 %constant_dynamic-slice_fusion.15 = (f32[1,1,1024,256]{3,2,1,0:T(8,128)S(1)}, f32[1,1,1024,256]{3,2,1,0:T(8,128)}, f32[1,1,1024,256]{3,2,1,0:T(8,128)}, f32[1,1,...) fusion(f32[3,2,1024,1024]{3,2,1,0:T(8,128)} %get-tuple-element.584, ...), kind=kLoop, calls=%fused_computation.102.clone.1 | loop fusion | bytes 12582924 | tf_op jit(solution)/shard_map/while/body/eval_jaxpr/slice | solution.py:87
  384.8 2.5 copy.70
  388.7 2.1 fusion.160
  390.8 2.5 copy.67
  393.3 2.5 copy.68
  404.2 84.1 %psum.7 = f32[4,1024]{1,0:T(4,128)S(1)} all-reduce(f32[4,1024]{1,0:T(4,128)S(1)} %bitcast.219), channel_id=1, replica_groups=mesh['ray'=16,'pix'=16] {'pix'}, use_global_device_ids=true, to_apply=%region_17.18 | all-reduce | flops 4096 | bytes 32768 | tf_op jit(solution)/shard_map/psum | solution.py:142
  (241 shorter events, 114.6 us)
Async XLA Ops:
  7.2 226.1 %reduce-scatter.4.cloned.1.call-start = ((), (), s32[]{:S(2)}) async-start(), calls=%async_computation.1 | async-start | bytes 1671168
  144.2 1.8 copy-start.6
  234.3 51.2 %copy-start.5 = (f32[64,384]{0,1:T(8,128)}, f32[64,384]{0,1:T(8,128)S(1)}, u32[]{:S(2)}) copy-start(f32[64,384]{0,1:T(8,128)S(1)} %copy.38) | copy-start | bytes 294916
  285.5 202.9 %copy-start.7 = (f32[2,1024]{1,0:T(2,128)S(1)}, f32[2,1024]{1,0:T(2,128)}, u32[]{:S(2)}) copy-start(f32[2,1024]{1,0:T(2,128)} %param.10) | copy-start | bytes 24580
  285.5 202.9 %copy-start.8 = (f32[2,1024]{1,0:T(2,128)S(1)}, f32[2,1024]{1,0:T(2,128)}, u32[]{:S(2)}) copy-start(f32[2,1024]{1,0:T(2,128)} %param.9) | copy-start | bytes 24580
  285.5 202.9 %copy-start.9 = (f32[1024]{0:T(1024)S(1)}, f32[1024]{0:T(1024)}, u32[]{:S(2)}) copy-start(f32[1024]{0:T(1024)} %param.12) | copy-start | bytes 12292
  306.8 1.8 copy-start.3
  306.8 2.3 copy-start.4
  311.4 1.4 copy-start
  311.4 1.5 copy-start.1
  311.4 1.8 copy-start.2
  336.5 1.8 copy-start.3
  336.5 2.3 copy-start.4
  341.1 1.4 copy-start
  341.1 1.5 copy-start.1
  341.1 1.8 copy-start.2
  366.2 1.8 copy-start.3
  366.2 2.3 copy-start.4
  370.8 1.4 copy-start
  370.8 1.5 copy-start.1
  370.8 1.8 copy-start.2
  395.9 1.8 copy-start.3
  395.9 2.3 copy-start.4
  400.4 1.4 copy-start
  400.4 1.5 copy-start.1
  400.5 1.8 copy-start.2
Sparse Core Ops, SparseCore 0:
  146.0 87.1 reduce-scatter.3
where the time goes:
time: 501 us; the launch traced here: 498 us
  blocking collectives  135 us (27%)
  other arithmetic  114 us (23%)
  local copies, waits for them, and re-layouts  98.7 us (20%)
  waiting for transfers between devices  87.3 us (17%)
  matrix products  44.4 us (9%)
  between operations  14.2 us (3%)
    unnamed x2, waiting for transfers between devices  87.3 us
    psum x1, blocking collectives, on_device(): sums = lax.psum(partial_value, 'pix')  84.1 us
    all_gather x1, blocking collectives, on_device(): gathered = lax.all_gather(grad_u, 'ray', axis=0, tiled=True)  51.1 us
    cos x1, other arithmetic, build_tables(): col_list.append(jnp.stack([jnp.cos(beta), jnp.sin(beta)]))  46.6 us
    dot_general x36, matrix products, product(): lax.dot_general(left, right, dims, preferred_element_type=jnp.float32)  44.4 us
    while x88, local copies, waits for them, and re-layouts  43.5 us
    slice x4, local copies, waits for them, and re-layouts, one_block(): b_re = b_blk[wave, 0]  20.6 us
    another operation x24, other arithmetic  16 us
  transfers between devices with their start and end apart: 1, of which 1 were waited for; matrix products, arithmetic and copies ran while one was open for 0% of the time, Pallas kernels for 0%

commit v1 on v0

--- a/solution.py
+++ b/solution.py
@@ -137,7 +137,9 @@
     row_tab, col_tab = build_tables(rays, rows_x, all_cols, norm)
     field = lax.psum_scatter(field_terms(row_tab, col_tab), "ray", scatter_dimension=0, tiled=True)
     psf, grad_u = intensity(field, psf_grad, clen, plen)
-    gathered = lax.all_gather(grad_u, "ray", axis=0, tiled=True)
+    gathered = jnp.concatenate(
+        lax.all_to_all(jnp.stack([grad_u] * lax.axis_size("ray")), "ray", 0, 0), axis=0
+    )
     partial_value = ray_partials(row_tab, col_tab, rows_x, all_cols, gathered)
     sums = lax.psum(partial_value, "pix")
     return (psf, finish(sums, rays))

time: 501 us -> 486 us (0.970)
  blocking collectives: 135 us -> 84.1 us
  matrix products: 44.4 us -> 60.3 us
  waiting for transfers between devices: 87.3 us -> 98.7 us
  starting transfers between devices: 0.04 us -> 9.38 us
    all_gather x1 -> x0, blocking collectives: 51.1 us -> none  [on_device(): gathered = lax.all_gather(grad_u, 'ray', axis=0, tiled=True)]
    dot_general x36, matrix products: 44.4 us -> 60.3 us  [product(): lax.dot_general(left, right, dims, preferred_element_type=jnp.float32)]
    all_to_all x0 -> x1, waiting for transfers between devices: none -> 11.8 us  [on_device(): lax.all_to_all(jnp.stack([grad_u] * lax.axis_size('ray')), 'ray', 0, 0)]
    all_to_all x0 -> x1, starting transfers between devices: none -> 9.34 us  [on_device(): lax.all_to_all(jnp.stack([grad_u] * lax.axis_size('ray')), 'ray', 0, 0)]
    while x88 -> x80, local copies, waits for them, and re-layouts: 43.5 us -> 41.8 us
    another operation x8 -> x9, local copies, waits for them, and re-layouts: 12.5 us -> 13.6 us
  transfers between devices with their start and end apart: 1 -> 2, of which waited for: 1 -> 2; matrix products, arithmetic and copies ran while one was open for 0% -> 0% of each run, Pallas kernels for 0% -> 0%
where the time goes in v1:
time: 486 us; the launch traced here: 482 us
  other arithmetic  114 us (23%)
  waiting for transfers between devices  98.7 us (20%)
  local copies, waits for them, and re-layouts  97.1 us (20%)
  blocking collectives  84.1 us (17%)
  matrix products  60.3 us (12%)
  between operations  14.2 us (3%)
  starting transfers between devices  9.38 us (2%)
    unnamed x2, waiting for transfers between devices  86.9 us
    psum x1, blocking collectives, on_device(): sums = lax.psum(partial_value, 'pix')  84.1 us
    dot_general x36, matrix products, product(): lax.dot_general(left, right, dims, preferred_element_type=jnp.float32)  60.3 us
    cos x1, other arithmetic, build_tables(): col_list.append(jnp.stack([jnp.cos(beta), jnp.sin(beta)]))  46.6 us
    while x80, local copies, waits for them, and re-layouts  41.8 us
    slice x4, local copies, waits for them, and re-layouts, one_block(): b_re = b_blk[wave, 0]  20.6 us
    another operation x24, other arithmetic  15.8 us
    unnamed x2, other arithmetic  15.7 us
  transfers between devices with their start and end apart: 2, of which 2 were waited for; matrix products, arithmetic and copies ran while one was open for 0% of the time, Pallas kernels for 0%

profile of v1, /device:TPU:32, one launch (start us, length us, event | category | flops | bytes accessed | tf_op | source)
XLA Modules:
  0.0 481.6 jit_solution(7906310572180617692)
XLA Ops:
  9.5 3.6 cosine_multiply_fusion.2
  13.2 46.6 %multiply_cosine_fusion.2 = (f32[1,1024,1024]{2,1,0:T(8,128)}, f32[1,1024,1024]{2,1,0:T(8,128)}, f32[1,1024,1024]{2,1,0:T(8,128)}, f32[1,1024,1024]{2,1,0:T(8,12...) fusion(f32[1024]{0:T(1024)S(1)} %bitcast.215, f32[1024]{0:T(1024)S(1)} %fusion.111, ...), kind=kLoop, calls=%fused_computation.186 | loop fusion | flops 3145728 | bytes 25182208 | tf_op jit(solution)/shard_map/cos | solution.py:32
  62.8 9.3 %maximum_bitcast_fusion.1 = (f32[1,2,1024,1024]{3,2,1,0:T(8,128)S(1)}, f32[1,2,1024,1024]{3,2,1,0:T(8,128)}) fusion(f32[1,1024,1024]{2,1,0:T(8,128)} %get-tuple-element.336, f32[1,1024,1024]{2,1,0:T(8,128)} %get-tuple-element.335, f32[1,1024,1024]{2,1,0:T(8,128)} %get-tuple-element.341, f32[1,1024,1024]{2,1,0:T(8,128)} %get-tuple-element.342), kind=kLoop, calls=%fused_computation.178 | loop fusion | flops 4194304 | bytes 33554432 | tf_op jit(solution)/shard_map/stack | solution.py:33
  72.1 15.7 %fusion.115 = (bf16[3,2,1024,1024]{3,2,1,0:T(8,128)(2,1)}, f32[3,2,1024,1024]{3,2,1,0:T(8,128)}) fusion(f32[1,2,1024,1024]{3,2,1,0:T(8,128)S(1)} %maximum_bitcast_fusion.3, f32[1,2,1024,1024]{3,2,1,0:T(8,128)} %get-tuple-element.346, f32[1,2,1024,1024]{3,2,1,0:T(8,128)S(1)} %get-tuple-element.345), kind=kLoop, calls=%fused_computation.219 | loop fusion | flops 18874368 | bytes 62914560
  87.8 56.3 %while.27 = (s32[]{:T(128)}, f32[1024,384]{0,1:T(8,128)S(1)}, bf16[3,2,1024,1024]{3,2,1,0:T(8,128)(2,1)}, f32[3,2,1024,64]{2,3,1,0:T(8,128)}, s32[]{:T(128)}, /*...) while((s32[]{:T(128)}, f32[1024,384]{0,1:T(8,128)S(1)}, bf16[3,2,1024,1024]{3,2,1,0:T(8,128)(2,1)}, ...), condition=%wide.region_1.0_spmd.clone, body=%wide.region_0.0_spmd.clone.sunk | while | flops 412237824 | bytes 23888080 | solution.py:67
  96.0 2.5 fusion.173
  110.1 2.5 fusion.173
  124.2 2.5 fusion.173
  138.2 2.5 fusion.173
  145.9 86.9 %reduce-scatter.4.cloned.1.call-done = f32[64,384]{1,0:T(8,128)} async-done(((f32[1024,384]{1,0:T(8,128)}), f32[64,384]{1,0:T(8,128)}) %reduce-scatter.4.cloned.1.call-update) | async-done | bytes 98320
  235.0 9.3 %all-to-all-start = ((bf16[16,64,384]{2,1,0:T(8,128)(2,1)}), bf16[16,64,384]{2,1,0:T(8,128)(2,1)}, u32[]{:S(2)}, u32[]{:S(2)}) async-start(bf16[16,64,384]{2,1,0:T(8,128)(2,1)} %stack.55), calls=%async_computation | async-start | bytes 1572864 | tf_op jit(solution)/shard_map/all_to_all | solution.py:141
  245.4 11.8 %all-to-all-done = bf16[16,64,384]{2,1,0:T(8,128)(2,1)} async-done(((bf16[16,64,384]{2,1,0:T(8,128)(2,1)}), bf16[16,64,384]{2,1,0:T(8,128)(2,1)}, u32[]{:S(2)}, u32[]{:S(2)}) %all-to-all-start) | async-done | bytes 786464 | tf_op jit(solution)/shard_map/all_to_all | solution.py:141
  257.2 132.7 %while.26 = (s32[]{:T(128)}, f32[4,4,256]{2,1,0:T(4,128)S(1)}, s32[4]{0:T(128)S(1)}, f32[3,2,1024,1024]{3,2,1,0:T(8,128)}, bf16[1024,384]{1,0:T(8,128)(2,1)}, /*...) while((s32[]{:T(128)}, f32[4,4,256]{2,1,0:T(4,128)S(1)}, ...), condition=%wide.region_16.17_spmd.clone.clone, body=%wide.region_3.16_spmd.clone.clone.sunk | while | flops 819468480 | bytes 76198768 | solution.py:104
  258.4 5.2 %constant_dynamic-slice_fusion.15 = (f32[1,1,1024,256]{3,2,1,0:T(8,128)S(1)}, f32[1,1,1024,256]{3,2,1,0:T(8,128)}, f32[1,1,1024,256]{3,2,1,0:T(8,128)}, f32[1,1,...) fusion(f32[3,2,1024,1024]{3,2,1,0:T(8,128)} %get-tuple-element.584, ...), kind=kLoop, calls=%fused_computation.102.clone.1 | loop fusion | bytes 12582924 | tf_op jit(solution)/shard_map/while/body/eval_jaxpr/slice | solution.py:87
  267.4 2.5 copy.70
  271.3 2.1 fusion.160
  273.5 2.5 copy.67
  276.0 2.5 copy.68
  291.6 5.2 %constant_dynamic-slice_fusion.15 = (f32[1,1,1024,256]{3,2,1,0:T(8,128)S(1)}, f32[1,1,1024,256]{3,2,1,0:T(8,128)}, f32[1,1,1024,256]{3,2,1,0:T(8,128)}, f32[1,1,...) fusion(f32[3,2,1024,1024]{3,2,1,0:T(8,128)} %get-tuple-element.584, ...), kind=kLoop, calls=%fused_computation.102.clone.1 | loop fusion | bytes 12582924 | tf_op jit(solution)/shard_map/while/body/eval_jaxpr/slice | solution.py:87
  300.6 2.5 copy.70
  304.5 2.1 fusion.160
  306.6 2.5 copy.67
  309.2 2.5 copy.68
  324.8 5.2 %constant_dynamic-slice_fusion.15 = (f32[1,1,1024,256]{3,2,1,0:T(8,128)S(1)}, f32[1,1,1024,256]{3,2,1,0:T(8,128)}, f32[1,1,1024,256]{3,2,1,0:T(8,128)}, f32[1,1,...) fusion(f32[3,2,1024,1024]{3,2,1,0:T(8,128)} %get-tuple-element.584, ...), kind=kLoop, calls=%fused_computation.102.clone.1 | loop fusion | bytes 12582924 | tf_op jit(solution)/shard_map/while/body/eval_jaxpr/slice | solution.py:87
  333.8 2.5 copy.70
  339.8 2.5 copy.67
  342.3 2.5 copy.68
  357.9 5.2 %constant_dynamic-slice_fusion.15 = (f32[1,1,1024,256]{3,2,1,0:T(8,128)S(1)}, f32[1,1,1024,256]{3,2,1,0:T(8,128)}, f32[1,1,1024,256]{3,2,1,0:T(8,128)}, f32[1,1,...) fusion(f32[3,2,1024,1024]{3,2,1,0:T(8,128)} %get-tuple-element.584, ...), kind=kLoop, calls=%fused_computation.102.clone.1 | loop fusion | bytes 12582924 | tf_op jit(solution)/shard_map/while/body/eval_jaxpr/slice | solution.py:87
  366.9 2.5 copy.70
  373.0 2.5 copy.67
  375.5 2.5 copy.68
  389.9 84.1 %psum.7 = f32[4,1024]{1,0:T(4,128)S(1)} all-reduce(f32[4,1024]{1,0:T(4,128)S(1)} %bitcast.220), channel_id=1, replica_groups=mesh['ray'=16,'pix'=16] {'pix'}, use_global_device_ids=true, to_apply=%region_17.18 | all-reduce | flops 4096 | bytes 32768 | tf_op jit(solution)/shard_map/psum | solution.py:144
  (233 shorter events, 130.9 us)
Async XLA Ops:
  7.2 225.7 %reduce-scatter.4.cloned.1.call-start = ((), (), s32[]{:S(2)}) async-start(), calls=%async_computation.2 | async-start | bytes 1671168
  144.2 1.7 copy-start.4
  235.0 22.1 %all-to-all-start = ((bf16[16,64,384]{2,1,0:T(8,128)(2,1)}), bf16[16,64,384]{2,1,0:T(8,128)(2,1)}, u32[]{:S(2)}, u32[]{:S(2)}) async-start(bf16[16,64,384]{2,1,0:T(8,128)(2,1)} %stack.55), calls=%async_computation | async-start | bytes 1572864 | tf_op jit(solution)/shard_map/all_to_all | solution.py:141
  257.2 216.8 %copy-start.5 = (f32[2,1024]{1,0:T(2,128)S(1)}, f32[2,1024]{1,0:T(2,128)}, u32[]{:S(2)}) copy-start(f32[2,1024]{1,0:T(2,128)} %param.10) | copy-start | bytes 24580
  257.2 216.8 %copy-start.6 = (f32[2,1024]{1,0:T(2,128)S(1)}, f32[2,1024]{1,0:T(2,128)}, u32[]{:S(2)}) copy-start(f32[2,1024]{1,0:T(2,128)} %param.9) | copy-start | bytes 24580
  257.2 216.9 %copy-start.7 = (f32[1024]{0:T(1024)S(1)}, f32[1024]{0:T(1024)}, u32[]{:S(2)}) copy-start(f32[1024]{0:T(1024)} %param.12) | copy-start | bytes 12292
  278.5 3.2 copy-start.3
  284.0 4.4 copy-start
  284.0 4.4 copy-start.1
  284.0 4.4 copy-start.2
  311.7 3.2 copy-start.3
  317.2 4.4 copy-start
  317.2 4.4 copy-start.1
  317.2 4.4 copy-start.2
  344.9 3.2 copy-start.3
  350.3 4.4 copy-start
  350.4 4.4 copy-start.1
  350.4 4.4 copy-start.2
  378.0 3.2 copy-start.3
  383.5 4.4 copy-start
  383.5 4.4 copy-start.1
  383.5 4.4 copy-start.2
Sparse Core Ops, SparseCore 0:
  146.0 86.7 reduce-scatter.3
